TPU v7x, 512 devices: a whole 4x8x8 slice. The times are simulated.
512 devices in a mesh: band: 64 (over x, y, z_hi), pw: 8 (over z_lo, core).
Axes of the slice: x: 4, y: 8, z: 8 (z_hi: 2, z_lo: 4; z = z_hi * 4 + z_lo), core: 2. Of those that a mesh axis runs over, the one named last changes fastest.
Arguments:
- occupied: bfloat16 [2, 64, 4096], P(None, 'pw'), may hold values from -6 to 6
- virtual: bfloat16 [64, 64, 4096], P('band', 'pw'), may hold values from -6 to 6
- screening: bfloat16 [16384, 16384], P('pw', 'band'), may hold values from -0.046875 to 0.046875
- grid_index: int32 [16384], replicated, may hold values from 0 to 262143, as said below
Outputs:
- grad_vir: float32 [64, 64, 4096], P('band', 'pw')
Inputs may be any that keep to these rules, and one draw needn't show every extreme that they name: `grid_index`: all entries are distinct. Write each entry as (kx * 64 + ky) * 64 + kz and take kx, ky, kz as signed frequencies (a value k of 32 or more stands for k - 64): every signed frequency lies within -16 to 16, and some entry has |kx| = |ky| = |kz| = 16. The entries g with g // 2048 = b are grid points whose ky is congruent to b modulo 64 // 8.
All inputs are finite; a program needn't handle non-finite values.
Results may differ from a plain program's by a relative error of at most 0.006.
Values may be sent and summed in bfloat16 or wider, within the bound.
A program may use at most 128 MiB of HBM per device.

v0:
```python
import math
import jax
import jax.numpy as jnp
from jax import lax
from jax.sharding import PartitionSpec as P

GRID = 64
NG = 16384
KMAX = 16
NK = 2 * KMAX + 1
PW = 8
BAND = 64
NJ = 5
PRECISE = lax.Precision.HIGHEST
F32 = jnp.float32
BF16 = jnp.bfloat16


def phases(left, right):
    angles = (left[:, None] * right[None, :] % GRID).astype(F32) * (2.0 * math.pi / GRID)
    return (jnp.cos(angles), jnp.sin(angles))


def dot(spec, a, b):
    return jnp.einsum(spec, a, b, precision=PRECISE, preferred_element_type=F32)


def body(occupied, virtual, screening, grid_index):
    pairs, planes = (occupied.shape[0], occupied.shape[1])
    slab = lax.axis_index("pw")
    cells = jnp.arange(GRID, dtype=jnp.int32)
    freqs = jnp.arange(NK, dtype=jnp.int32) - KMAX
    row_freqs = (
        jnp.arange(PW, dtype=jnp.int32)[:, None] - KMAX + PW * jnp.arange(NJ, dtype=jnp.int32)[None]
    )
    cos_k, sin_k = phases(cells, freqs)
    cos_y, sin_y = phases(cells, row_freqs.reshape(-1))
    block = NG // PW
    own = lax.dynamic_slice_in_dim(grid_index, slab * block, block)

    def signed(k):
        return jnp.where(k >= GRID // 2, k - GRID, k)

    at_x = signed(own // (GRID * GRID)) + KMAX
    at_j = (signed(own // GRID % GRID) + KMAX - slab) // PW
    at_z = signed(own % GRID) + KMAX
    at_jz = at_j * NK + at_z
    pick_x = (jnp.arange(NK, dtype=jnp.int32)[:, None] == at_x[None]).astype(BF16)
    pick_jz = jnp.arange(NJ * NK, dtype=jnp.int32)[:, None] == at_jz[None]
    density = occupied.astype(F32) * virtual.astype(F32)
    density = density.reshape(pairs, planes, GRID, GRID)
    forward_z = jnp.concatenate([cos_k, -sin_k], axis=1)
    field = dot("pxyz,zc->pxyc", density, forward_z)
    both_y = jnp.concatenate([cos_y, sin_y], axis=1)
    mixed = dot("pxyc,yk->pxkc", field, both_y).reshape(pairs, planes, 2, PW, NJ, 2, NK)
    real = mixed[:, :, 0, :, :, 0] + mixed[:, :, 1, :, :, 1]
    imag = mixed[:, :, 0, :, :, 1] - mixed[:, :, 1, :, :, 0]
    field = jnp.stack([real, imag], axis=0).astype(BF16)
    field = field.transpose(3, 2, 1, 0, 4, 5).reshape(PW, planes, pairs * 2 * NJ * NK)
    pencil = lax.all_to_all(field, "pw", 0, 0, tiled=True).reshape(GRID, -1)
    cos_sin = jnp.concatenate([cos_k, sin_k], axis=1)
    mixed = dot("xm,xk->mk", pencil.astype(F32), cos_sin).reshape(pairs, 2, NJ * NK, 2, NK)
    real = mixed[:, 0, :, 0] + mixed[:, 1, :, 1]
    imag = mixed[:, 1, :, 0] - mixed[:, 0, :, 1]
    box = (jnp.stack([real, imag], axis=1) * (1.0 / math.sqrt(GRID**3))).astype(BF16)
    columns = jnp.einsum("prmk,kg->prmg", box, pick_x, preferred_element_type=F32)
    spectra = jnp.sum(jnp.where(pick_jz[None, None], columns, 0.0), axis=2).astype(BF16)
    rows = pairs * 2
    everyone = lax.all_gather(spectra.reshape(rows, block), "band", axis=0, tiled=True)
    partial = jnp.dot(everyone, screening, preferred_element_type=F32).astype(BF16)
    width = screening.shape[1]
    partial = lax.all_to_all(partial.reshape(PW, PW * rows, width), "pw", 0, 0, tiled=True)
    summed = jnp.sum(partial.astype(F32), axis=0).astype(BF16).reshape(PW, rows, width)
    turn = []
    for c1 in range(PW):
        for c0 in range(PW):
            for p in range(PW):
                turn.append(((c1 * PW + c0) * PW + p, (p * PW + c0) * PW + c1))
    summed = lax.ppermute(summed, ("band", "pw"), turn)
    groups = [[PW * k + t for t in range(PW)] for k in range(BAND // PW)]
    home = lax.all_to_all(summed, "band", 0, 0, axis_index_groups=groups, tiled=True)
    screened = home.transpose(1, 0, 2).reshape(rows, 1, block)
    spread = jnp.where(pick_jz[None], screened, jnp.zeros((), BF16)).reshape(rows * NJ * NK, block)
    box = jnp.einsum("mg,kg->mk", spread, pick_x, preferred_element_type=F32)
    mixed = dot("xk,mk->xm", jnp.concatenate([cos_k, sin_k], axis=0), box)
    mixed = mixed.reshape(2, GRID, pairs, 2, NJ * NK)
    real = mixed[0, :, :, 0] - mixed[1, :, :, 1]
    imag = mixed[0, :, :, 1] + mixed[1, :, :, 0]
    pencil = jnp.stack([real, imag], axis=2).astype(BF16).reshape(PW, planes, -1)
    field = lax.all_to_all(pencil, "pw", 0, 0, tiled=True)
    field = field.reshape(PW, planes, pairs, 2, NJ, NK).astype(F32)
    field = field.transpose(2, 1, 0, 4, 3, 5).reshape(pairs, planes, PW * NJ, 2 * NK)
    mixed = dot("pxkc,yk->pxyc", field, jnp.concatenate([cos_y, sin_y], axis=0))
    mixed = mixed.reshape(pairs, planes, 2, GRID, 2 * NK)
    mixed = jnp.concatenate([mixed[:, :, 0], mixed[:, :, 1]], axis=-1)
    cz, sz = (jnp.transpose(cos_k), jnp.transpose(sin_k))
    back = jnp.concatenate([cz, -sz, -sz, -cz], axis=0) * (1.0 / math.sqrt(NG))
    potential = dot("pxyc,cz->pxyz", mixed, back)
    weighted = potential.reshape(pairs, planes, GRID * GRID) * occupied.astype(F32)
    return jnp.sum(weighted, axis=0)[None]


def solution(mesh):
    return jax.shard_map(
        body,
        mesh=mesh,
        in_specs=(P(None, "pw", None), P("band", "pw", None), P("pw", "band"), P()),
        out_specs=P("band", "pw", None),
        check_vma=False,
    )
```

profile of v0, /device:TPU:1, one launch (start us, length us, event | category | flops | bytes accessed | tf_op | source)
XLA Modules:
  0.0 234.0 jit_solution(1686862326288065486)
XLA Ops:
  6.5 0.0 copy-start
  6.5 0.2 fusion.68
  6.7 0.9 bitcast_convert_fusion
  7.7 0.9 convert_multiply_fusion.1
  8.6 0.2 reshape.230
  8.8 0.1 broadcast_add_fusion
  8.9 0.1 add.166
  9.0 0.2 fusion.71
  9.2 0.6 fusion.37
  9.7 1.1 convolution_bitcast_fusion.1
  10.9 0.3 copy.91
  11.1 0.8 reshape.231
  11.9 1.0 fusion.90
  12.9 0.1 fusion.10
  13.0 0.1 maximum_bitcast_fusion
  13.1 0.1 copy.96
  13.2 1.2 reshape.232
  14.4 10.1 %all-to-all-start = ((bf16[8,8,660]{2,1,0:T(8,128)(2,1)}), bf16[8,8,660]{2,1,0:T(8,128)(2,1)S(1)}, u32[]{:S(2)}, u32[]{:S(2)}) async-start(bf16[8,8,660]{2,1,0:T(8,128)(2,1)} %reshape.232), calls=%async_computation | async-start | bytes 196608 | tf_op jit(solution)/shard_map/all_to_all | solution.py:60
  24.5 0.0 all-gather.3.cloned.1.call-start
  24.5 0.7 fusion.80
  25.2 0.7 fusion.75
  25.9 0.2 iota_compare_fusion
  26.2 3.7 %all-to-all-done = bf16[8,8,660]{2,1,0:T(8,128)(2,1)S(1)} async-done(((bf16[8,8,660]{2,1,0:T(8,128)(2,1)}), bf16[8,8,660]{2,1,0:T(8,128)(2,1)S(1)}, u32[]{:S(2)}, u32[]{:S(2)}) %all-to-all-start) | async-done | bytes 84512 | tf_op jit(solution)/shard_map/all_to_all | solution.py:60
  29.9 0.1 dot_general.38
  30.0 0.3 fusion.17
  30.4 1.0 select_reduce_fusion
  31.4 0.6 reshape.242
  32.0 0.0 all-gather.3.cloned.1.call-update
  32.0 127.1 %all-gather.3.cloned.1.call-done = bf16[64,4,2048]{2,1,0:T(4,128)(2,1)} async-done(((bf16[1,4,2048]{2,1,0:T(4,128)(2,1)}), bf16[64,4,2048]{2,1,0:T(4,128)(2,1)}) %all-gather.3.cloned.1.call-update) | async-done | bytes 1048592 | tf_op jit(solution)/shard_map/all_gather | solution.py:69
  159.1 1.3 reshape.243
  160.5 0.0 copy-done
  160.5 0.4 convolution_convert_fusion
  160.9 13.9 %all_to_all.20 = bf16[8,32,256]{2,1,0:T(8,128)(2,1)S(1)} all-to-all(bf16[8,32,256]{2,1,0:T(8,128)(2,1)S(1)} %bitcast.87), channel_id=1, replica_groups=mesh['band'=64,'pw'=8] {'pw'}, dimensions={0} | all-to-all | bytes 262144 | tf_op jit(solution)/shard_map/all_to_all | solution.py:72
  174.9 4.9 %collective-permute-start = (bf16[8,4,256]{2,1,0:T(4,128)(2,1)S(1)}, bf16[8,4,256]{2,1,0:T(4,128)(2,1)S(1)}, u32[]{:S(2)}, u32[]{:S(2)}) collective-permute-start(bf16[8,4,256]{2,1,0:T(4,128)(2,1)S(1)} %reshape.235), channel_id=1, source_target_pairs={{0,0},{1,64},{2,128},{3,192},{4,256},{5,320},{6,384},{7,448},{8,8}... | collective-permute-start | bytes 49160 | tf_op jit(solution)/shard_map/ppermute | solution.py:79
  179.8 4.1 %collective-permute-done = bf16[8,4,256]{2,1,0:T(4,128)(2,1)S(1)} collective-permute-done((bf16[8,4,256]{2,1,0:T(4,128)(2,1)S(1)}, bf16[8,4,256]{2,1,0:T(4,128)(2,1)S(1)}, u32[]{:S(2)}, u32[]{:S(2)}) %collective-permute-start) | collective-permute-done | bytes 16416 | tf_op jit(solution)/shard_map/ppermute | solution.py:79
  183.8 12.4 %all_to_all.21 = bf16[8,4,256]{2,1,0:T(4,128)(2,1)S(1)} all-to-all(bf16[8,4,256]{2,1,0:T(4,128)(2,1)S(1)} %collective-permute-done), channel_id=1, replica_groups={{0,8,16,24,32,40,48,56},{64,72,80,88,96,104,112,120},{128,136,144,152,1..., dimensions={0} | all-to-all | bytes 32768 | tf_op jit(solution)/shard_map/all_to_all | solution.py:81
  196.3 2.0 broadcast_select_fusion
  198.2 4.1 %select_n.97 = bf16[660,2048]{1,0:T(8,128)(2,1)} reshape(bf16[4,165,2048]{2,1,0:T(8,128)(2,1)} %broadcast_select_fusion) | data formatting | bytes 5406720 | tf_op jit(solution)/shard_map/jit(_where)/select_n | solution.py:83
  202.3 2.7 %fusion.6 = f32[660,33]{0,1:T(8,128)S(1)} fusion(bf16[660,2048]{1,0:T(8,128)(2,1)} %select_n.97, s32[2048]{0:T(1024)S(1)} %get-tuple-element.5), kind=kOutput, calls=%fused_computation.18 | convolution fusion | flops 89278464 | bytes 2798672 | tf_op jit(solution)/shard_map/mg,kg->mk/dot_general | solution.py:84
  205.0 0.6 fusion.56
  205.6 0.8 reshape.236
  206.4 0.4 fusion.92
  206.9 0.1 copy.106
  207.0 0.8 convert_element_type.68
  207.8 7.9 %all-to-all-start.3 = ((bf16[8,8,660]{2,1,0:T(8,128)(2,1)}), bf16[8,8,660]{2,1,0:T(8,128)(2,1)S(1)}, u32[]{:S(2)}, u32[]{:S(2)}) async-start(bf16[8,8,660]{2,1,0:T(8,128)(2,1)} %convert_element_type.68), calls=%async_computation.3 | async-start | bytes 196608 | tf_op jit(solution)/shard_map/all_to_all | solution.py:90
  215.7 0.2 fusion.66
  215.9 5.2 %all-to-all-done.3 = bf16[8,8,660]{2,1,0:T(8,128)(2,1)S(1)} async-done(((bf16[8,8,660]{2,1,0:T(8,128)(2,1)}), bf16[8,8,660]{2,1,0:T(8,128)(2,1)S(1)}, u32[]{:S(2)}, u32[]{:S(2)}) %all-to-all-start.3) | async-done | bytes 84512 | tf_op jit(solution)/shard_map/all_to_all | solution.py:90
  221.1 0.9 reshape.237
  222.0 0.3 copy.107
  222.3 0.2 reshape.238
  222.5 0.5 convolution_bitcast_fusion
  223.0 0.6 reshape.253
  223.6 0.8 fusion.91
  224.4 0.0 copy-start.1
  224.4 0.4 copy.135
  224.8 0.4 copy.136
  225.2 1.1 fusion
  226.3 0.2 reshape.240
  226.5 0.0 copy-done.1
  226.5 0.7 fusion.9
  (12 shorter events, 0.1 us)
Async XLA Ops:
  6.5 153.9 %copy-start = (bf16[2048,256]{1,0:T(8,128)(2,1)S(1)}, bf16[2048,256]{1,0:T(8,128)(2,1)}, u32[]{:S(2)}) copy-start(bf16[2048,256]{1,0:T(8,128)(2,1)} %param.6) | copy-start | bytes 3145732
  14.4 15.5 %all-to-all-start = ((bf16[8,8,660]{2,1,0:T(8,128)(2,1)}), bf16[8,8,660]{2,1,0:T(8,128)(2,1)S(1)}, u32[]{:S(2)}, u32[]{:S(2)}) async-start(bf16[8,8,660]{2,1,0:T(8,128)(2,1)} %reshape.232), calls=%async_computation | async-start | bytes 196608 | tf_op jit(solution)/shard_map/all_to_all | solution.py:60
  24.5 134.6 %all-gather.3.cloned.1.call-start = ((), (), s32[]{:S(2)}) async-start(), calls=%async_computation.4 | async-start | bytes 1064960 | tf_op jit(solution)/shard_map/all_gather | solution.py:69
  174.9 9.0 %collective-permute-start = (bf16[8,4,256]{2,1,0:T(4,128)(2,1)S(1)}, bf16[8,4,256]{2,1,0:T(4,128)(2,1)S(1)}, u32[]{:S(2)}, u32[]{:S(2)}) collective-permute-start(bf16[8,4,256]{2,1,0:T(4,128)(2,1)S(1)} %reshape.235), channel_id=1, source_target_pairs={{0,0},{1,64},{2,128},{3,192},{4,256},{5,320},{6,384},{7,448},{8,8}... | collective-permute-start | bytes 49160 | tf_op jit(solution)/shard_map/ppermute | solution.py:79
  207.8 13.3 %all-to-all-start.3 = ((bf16[8,8,660]{2,1,0:T(8,128)(2,1)}), bf16[8,8,660]{2,1,0:T(8,128)(2,1)S(1)}, u32[]{:S(2)}, u32[]{:S(2)}) async-start(bf16[8,8,660]{2,1,0:T(8,128)(2,1)} %convert_element_type.68), calls=%async_computation.3 | async-start | bytes 196608 | tf_op jit(solution)/shard_map/all_to_all | solution.py:90
  224.4 2.1 copy-start.1
Sparse Core Ops, SparseCore 0:
  32.2 126.9 all-gather.2
where the time goes:
time: 235 us; the launch traced here: 234 us
  waiting for transfers between devices  140 us (60%)
  blocking collectives  26.3 us (11%)
  starting transfers between devices  22.9 us (10%)
  local copies, waits for them, and re-layouts  15.7 us (7%)
  between operations  13.7 us (6%)
  matrix products  8.27 us (4%)
  other arithmetic  7 us (3%)
    all_gather x1, waiting for transfers between devices, body(): lax.all_gather(spectra.reshape(rows, block), 'band', axis=0, tiled=True)  127 us
    all_to_all x1, blocking collectives, body(): lax.all_to_all(partial.reshape(PW, PW * rows, width), 'pw', 0, 0, tiled=T...  13.9 us
    all_to_all x1, blocking collectives, body(): lax.all_to_all(summed, 'band', 0, 0, axis_index_groups=groups, tiled=True)  12.4 us
    all_to_all x1, starting transfers between devices, body(): pencil = lax.all_to_all(field, 'pw', 0, 0, tiled=True).reshape(GRID, -1)  10.1 us
    all_to_all x1, starting transfers between devices, body(): field = lax.all_to_all(pencil, 'pw', 0, 0, tiled=True)  7.91 us
    all_to_all x1, waiting for transfers between devices, body(): field = lax.all_to_all(pencil, 'pw', 0, 0, tiled=True)  5.21 us
    ppermute x1, starting transfers between devices, body(): summed = lax.ppermute(summed, ('band', 'pw'), turn)  4.9 us
  transfers between devices with their start and end apart: 4, of which 4 were waited for; matrix products, arithmetic and copies ran while one was open for 1% of the time, Pallas kernels for 0%

commit v1 on v0

--- a/solution.py
+++ b/solution.py
@@ -66,7 +66,15 @@
     columns = jnp.einsum("prmk,kg->prmg", box, pick_x, preferred_element_type=F32)
     spectra = jnp.sum(jnp.where(pick_jz[None, None], columns, 0.0), axis=2).astype(BF16)
     rows = pairs * 2
-    everyone = lax.all_gather(spectra.reshape(rows, block), "band", axis=0, tiled=True)
+    everyone = jnp.concatenate(
+        lax.all_to_all(
+            jnp.stack([spectra.reshape(rows, block)] * lax.axis_size("band")),
+            "band",
+            split_axis=0,
+            concat_axis=0,
+        ),
+        axis=0,
+    )
     partial = jnp.dot(everyone, screening, preferred_element_type=F32).astype(BF16)
     width = screening.shape[1]
     partial = lax.all_to_all(partial.reshape(PW, PW * rows, width), "pw", 0, 0, tiled=True)

time: 235 us -> 136 us (0.58)
  waiting for transfers between devices: 140 us -> 12.4 us
  blocking collectives: 26.3 us -> 69.2 us
  between operations: 13.7 us -> 0.4 us
    all_gather x1 -> x0, waiting for transfers between devices: 127 us -> none  [body(): lax.all_gather(spectra.reshape(rows, block), 'band', axis=0, tiled=True)]
    all_to_all x0 -> x1, blocking collectives: none -> 45.2 us  [body(): lax.all_to_all(jnp.stack([spectra.reshape(rows, block)] * lax.axis_size('...]
    all_to_all x1, blocking collectives: 13.9 us -> 11.2 us  [body(): lax.all_to_all(partial.reshape(PW, PW * rows, width), 'pw', 0, 0, tiled=T...]
  transfers between devices with their start and end apart: 4 -> 3, of which waited for: 4 -> 3; matrix products, arithmetic and copies ran while one was open for 1% -> 1% of each run, Pallas kernels for 0% -> 0%
where the time goes in v1:
time: 136 us; the launch traced here: 135 us
  blocking collectives  69.2 us (51%)
  starting transfers between devices  23.3 us (17%)
  local copies, waits for them, and re-layouts  14.6 us (11%)
  waiting for transfers between devices  12.4 us (9%)
  matrix products  8.26 us (6%)
  other arithmetic  7.01 us (5%)
    all_to_all x1, blocking collectives, body(): lax.all_to_all(jnp.stack([spectra.reshape(rows, block)] * lax.axis_size('...  45.2 us
    all_to_all x1, blocking collectives, body(): lax.all_to_all(summed, 'band', 0, 0, axis_index_groups=groups, tiled=True)  12.8 us
    all_to_all x1, blocking collectives, body(): lax.all_to_all(partial.reshape(PW, PW * rows, width), 'pw', 0, 0, tiled=T...  11.2 us
    all_to_all x1, starting transfers between devices, body(): pencil = lax.all_to_all(field, 'pw', 0, 0, tiled=True).reshape(GRID, -1)  10.1 us
    all_to_all x1, starting transfers between devices, body(): field = lax.all_to_all(pencil, 'pw', 0, 0, tiled=True)  7.74 us
    ppermute x1, starting transfers between devices, body(): summed = lax.ppermute(summed, ('band', 'pw'), turn)  5.47 us
    all_to_all x1, waiting for transfers between devices, body(): field = lax.all_to_all(pencil, 'pw', 0, 0, tiled=True)  5.21 us
    dot_general x6, matrix products, dot(): return jnp.einsum(spec, a, b, precision=PRECISE, preferred_element_type=F32)  4.12 us
  transfers between devices with their start and end apart: 3, of which 3 were waited for; matrix products, arithmetic and copies ran while one was open for 1% of the time, Pallas kernels for 0%

profile of v1, /device:TPU:1, one launch (start us, length us, event | category | flops | bytes accessed | tf_op | source)
XLA Modules:
  0.0 135.2 jit_solution(6816391122266474367)
XLA Ops:
  0.0 0.0 copy-start
  0.0 0.2 fusion.68
  0.2 0.9 bitcast_convert_fusion
  1.1 0.9 convert_multiply_fusion.1
  2.1 0.2 reshape.234
  2.3 0.1 broadcast_add_fusion
  2.4 0.1 add.166
  2.5 0.2 fusion.71
  2.6 0.0 copy-start.2
  2.6 0.6 fusion.37
  3.2 1.1 convolution_bitcast_fusion.1
  4.3 0.0 copy-done.2
  4.4 0.3 copy.91
  4.6 0.8 reshape.235
  5.4 1.0 fusion.90
  6.4 0.1 fusion.10
  6.5 0.1 maximum_bitcast_fusion
  6.6 0.1 copy.96
  6.7 1.2 reshape.236
  7.9 10.1 %all-to-all-start = ((bf16[8,8,660]{2,1,0:T(8,128)(2,1)}), bf16[8,8,660]{2,1,0:T(8,128)(2,1)S(1)}, u32[]{:S(2)}, u32[]{:S(2)}) async-start(bf16[8,8,660]{2,1,0:T(8,128)(2,1)} %reshape.236), calls=%async_computation | async-start | bytes 196608 | tf_op jit(solution)/shard_map/all_to_all | solution.py:60
  18.0 0.7 fusion.80
  18.7 0.0 copy-start.4
  18.7 0.7 fusion.75
  19.4 0.2 iota_compare_fusion
  19.7 3.7 %all-to-all-done = bf16[8,8,660]{2,1,0:T(8,128)(2,1)S(1)} async-done(((bf16[8,8,660]{2,1,0:T(8,128)(2,1)}), bf16[8,8,660]{2,1,0:T(8,128)(2,1)S(1)}, u32[]{:S(2)}, u32[]{:S(2)}) %all-to-all-start) | async-done | bytes 84512 | tf_op jit(solution)/shard_map/all_to_all | solution.py:60
  23.4 0.1 dot_general.38
  23.5 0.3 fusion.17
  23.8 1.0 select_reduce_fusion
  24.9 0.0 copy-done.4
  24.9 0.5 stack.22
  25.4 45.2 %all_to_all.25 = bf16[64,4,2048]{2,1,0:T(4,128)(2,1)S(1)} all-to-all(bf16[64,4,2048]{2,1,0:T(4,128)(2,1)S(1)} %stack.22), channel_id=1, replica_groups=mesh['band'=64,'pw'=8] {'band'}, dimensions={0} | all-to-all | bytes 2097152 | tf_op jit(solution)/shard_map/all_to_all | solution.py:70
  70.6 0.3 reshape.238
  70.9 0.0 copy-done
  70.9 0.4 convolution_convert_fusion
  71.3 11.2 %all_to_all.26 = bf16[8,32,256]{2,1,0:T(8,128)(2,1)S(1)} all-to-all(bf16[8,32,256]{2,1,0:T(8,128)(2,1)S(1)} %bitcast.87), channel_id=1, replica_groups=mesh['band'=64,'pw'=8] {'pw'}, dimensions={0} | all-to-all | bytes 262144 | tf_op jit(solution)/shard_map/all_to_all | solution.py:80
  82.6 5.5 %collective-permute-start = (bf16[8,4,256]{2,1,0:T(4,128)(2,1)S(1)}, bf16[8,4,256]{2,1,0:T(4,128)(2,1)S(1)}, u32[]{:S(2)}, u32[]{:S(2)}) collective-permute-start(bf16[8,4,256]{2,1,0:T(4,128)(2,1)S(1)} %reshape.240), channel_id=1, source_target_pairs={{0,0},{1,64},{2,128},{3,192},{4,256},{5,320},{6,384},{7,448},{8,8}... | collective-permute-start | bytes 49160 | tf_op jit(solution)/shard_map/ppermute | solution.py:87
  88.0 3.5 %collective-permute-done = bf16[8,4,256]{2,1,0:T(4,128)(2,1)S(1)} collective-permute-done((bf16[8,4,256]{2,1,0:T(4,128)(2,1)S(1)}, bf16[8,4,256]{2,1,0:T(4,128)(2,1)S(1)}, u32[]{:S(2)}, u32[]{:S(2)}) %collective-permute-start) | collective-permute-done | bytes 16416 | tf_op jit(solution)/shard_map/ppermute | solution.py:87
  91.5 12.8 %all_to_all.27 = bf16[8,4,256]{2,1,0:T(4,128)(2,1)S(1)} all-to-all(bf16[8,4,256]{2,1,0:T(4,128)(2,1)S(1)} %collective-permute-done), channel_id=1, replica_groups={{0,8,16,24,32,40,48,56},{64,72,80,88,96,104,112,120},{128,136,144,152,1..., dimensions={0} | all-to-all | bytes 32768 | tf_op jit(solution)/shard_map/all_to_all | solution.py:89
  104.4 2.0 %broadcast_select_fusion = bf16[4,165,2048]{2,1,0:T(8,128)(2,1)} fusion(pred[165,2048]{1,0:T(8,128)(4,1)S(1)} %iota_compare_fusion, bf16[4,2048]{1,0:T(4,128)(2,1)S(1)} %bitcast.90), kind=kLoop, calls=%fused_computation.1 | loop fusion | flops 1351680 | bytes 3057664 | tf_op jit(solution)/shard_map/jit(_where)/select_n | solution.py:91
  106.3 4.1 %select_n.97 = bf16[660,2048]{1,0:T(8,128)(2,1)} reshape(bf16[4,165,2048]{2,1,0:T(8,128)(2,1)} %broadcast_select_fusion) | data formatting | bytes 5406720 | tf_op jit(solution)/shard_map/jit(_where)/select_n | solution.py:91
  110.4 0.0 copy-done.5
  110.4 2.7 %fusion.6 = f32[660,33]{0,1:T(8,128)S(1)} fusion(bf16[660,2048]{1,0:T(8,128)(2,1)} %select_n.97, s32[2048]{0:T(1024)S(1)} %copy-done.5), kind=kOutput, calls=%fused_computation.18 | convolution fusion | flops 89278464 | bytes 2798672 | tf_op jit(solution)/shard_map/mg,kg->mk/dot_general | solution.py:92
  113.1 0.6 fusion.56
  113.7 0.0 copy-start.3
  113.7 0.8 reshape.241
  114.6 0.4 fusion.92
  115.1 0.1 copy.106
  115.2 0.8 convert_element_type.69
  116.0 7.7 %all-to-all-start.4 = ((bf16[8,8,660]{2,1,0:T(8,128)(2,1)}), bf16[8,8,660]{2,1,0:T(8,128)(2,1)S(1)}, u32[]{:S(2)}, u32[]{:S(2)}) async-start(bf16[8,8,660]{2,1,0:T(8,128)(2,1)} %convert_element_type.69), calls=%async_computation.4 | async-start | bytes 196608 | tf_op jit(solution)/shard_map/all_to_all | solution.py:98
  123.7 0.2 fusion.66
  123.9 5.2 %all-to-all-done.4 = bf16[8,8,660]{2,1,0:T(8,128)(2,1)S(1)} async-done(((bf16[8,8,660]{2,1,0:T(8,128)(2,1)}), bf16[8,8,660]{2,1,0:T(8,128)(2,1)S(1)}, u32[]{:S(2)}, u32[]{:S(2)}) %all-to-all-start.4) | async-done | bytes 84512 | tf_op jit(solution)/shard_map/all_to_all | solution.py:98
  129.1 0.9 reshape.242
  130.0 0.3 copy.107
  130.3 0.2 reshape.243
  130.5 0.0 copy-done.3
  130.5 0.5 convolution_bitcast_fusion
  131.0 0.6 reshape.255
  131.6 0.8 fusion.91
  132.5 0.0 copy-start.1
  132.5 0.4 copy.135
  132.9 0.4 copy.136
  133.3 1.1 fusion
  134.3 0.2 reshape.245
  134.5 0.7 fusion.9
  (15 shorter events, 0.2 us)
Async XLA Ops:
  0.0 70.9 %copy-start = (bf16[2048,256]{1,0:T(8,128)(2,1)S(1)}, bf16[2048,256]{1,0:T(8,128)(2,1)}, u32[]{:S(2)}) copy-start(bf16[2048,256]{1,0:T(8,128)(2,1)} %param.6) | copy-start | bytes 3145732
  2.6 1.7 %copy-start.2 = (f32[64,40]{0,1:T(8,128)}, f32[64,40]{0,1:T(8,128)S(1)}, u32[]{:S(2)}) copy-start(f32[64,40]{0,1:T(8,128)S(1)} %get-tuple-element.24) | copy-start | bytes 30724
  7.9 15.5 %all-to-all-start = ((bf16[8,8,660]{2,1,0:T(8,128)(2,1)}), bf16[8,8,660]{2,1,0:T(8,128)(2,1)S(1)}, u32[]{:S(2)}, u32[]{:S(2)}) async-start(bf16[8,8,660]{2,1,0:T(8,128)(2,1)} %reshape.236), calls=%async_computation | async-start | bytes 196608 | tf_op jit(solution)/shard_map/all_to_all | solution.py:60
  18.7 6.2 %copy-start.4 = (s32[2048]{0:T(1024)}, s32[2048]{0:T(1024)S(1)}, u32[]{:S(2)}) copy-start(s32[2048]{0:T(1024)S(1)} %get-tuple-element.5) | copy-start | bytes 24580
  82.6 9.0 %collective-permute-start = (bf16[8,4,256]{2,1,0:T(4,128)(2,1)S(1)}, bf16[8,4,256]{2,1,0:T(4,128)(2,1)S(1)}, u32[]{:S(2)}, u32[]{:S(2)}) collective-permute-start(bf16[8,4,256]{2,1,0:T(4,128)(2,1)S(1)} %reshape.240), channel_id=1, source_target_pairs={{0,0},{1,64},{2,128},{3,192},{4,256},{5,320},{6,384},{7,448},{8,8}... | collective-permute-start | bytes 49160 | tf_op jit(solution)/shard_map/ppermute | solution.py:87
  106.3 4.1 %copy-start.5 = (s32[2048]{0:T(1024)S(1)}, s32[2048]{0:T(1024)}, u32[]{:S(2)}) copy-start(s32[2048]{0:T(1024)} %copy-done.4) | copy-start | bytes 24580
  113.7 16.7 %copy-start.3 = (f32[64,40]{0,1:T(8,128)S(1)}, f32[64,40]{0,1:T(8,128)}, u32[]{:S(2)}) copy-start(f32[64,40]{0,1:T(8,128)} %copy-done.2) | copy-start | bytes 30724
  116.0 13.1 %all-to-all-start.4 = ((bf16[8,8,660]{2,1,0:T(8,128)(2,1)}), bf16[8,8,660]{2,1,0:T(8,128)(2,1)S(1)}, u32[]{:S(2)}, u32[]{:S(2)}) async-start(bf16[8,8,660]{2,1,0:T(8,128)(2,1)} %convert_element_type.69), calls=%async_computation.4 | async-start | bytes 196608 | tf_op jit(solution)/shard_map/all_to_all | solution.py:98
  132.5 2.1 %copy-start.1 = (bf16[2,8,4096]{2,1,0:T(8,128)(2,1)S(1)}, bf16[2,8,4096]{2,1,0:T(8,128)(2,1)}, u32[]{:S(2)}) copy-start(bf16[2,8,4096]{2,1,0:T(8,128)(2,1)} %param.4) | copy-start | bytes 393220
